TPU v7x, 32 devices: a whole 2x2x4 slice. The times are simulated.
32 devices in a mesh: dp: 8 (over z, x), tensor: 4 (over y, core).
Axes of the slice: x: 2, y: 2, z: 4, core: 2. Of those that a mesh axis runs over, the one named last changes fastest.
Arguments:
- tokens: bfloat16 [512, 4096], P('dp', 'tensor')
- norm_gain: float32 [4096], P('tensor'), may hold values from 0.5 to 1.5
- eraser_mean: float32 [4096], P('tensor'), may hold values from -6 to 6
- eraser_in: float32 [4096, 128], P('tensor'), may hold values from -0.09375 to 0.09375
- eraser_out: float32 [4096, 128], P('tensor'), may hold values from -0.5 to 0.5
- router: float32 [4096, 8], P('tensor'), may hold values from -0.09375 to 0.09375
- expert_ids: int32 [512, 2], P('dp'), may hold values from 0 to 7, as said below
- slots: int32 [512, 2], P('dp'), may hold values from 0 to 63, as said below
- w_gate: bfloat16 [8, 4096, 14336], P('dp', None, 'tensor'), may hold values from -0.09375 to 0.09375
- w_up: bfloat16 [8, 4096, 14336], P('dp', None, 'tensor'), may hold values from -0.09375 to 0.09375
- w_down: bfloat16 [8, 14336, 4096], P('dp', 'tensor'), may hold values from -0.0625 to 0.0625
Outputs:
- moe_out: bfloat16 [512, 4096], P('dp', 'tensor')
Inputs may be any that keep to these rules, and one draw needn't show every extreme that they name: `expert_ids`: the two experts of a token differ. Within each aligned block of 64 tokens, the choices naming one expert have the slots 0, 1, 2, ... with no repeats; choices with a slot of 24 or more are dropped.
All inputs are finite; a program needn't handle non-finite values.
Results may differ from a plain program's by a relative error of at most 0.0065.
Values may be sent and summed in bfloat16 or wider, within the bound.
A program may use at most 128 MiB of HBM per device.

v0:
```python
import jax
import jax.numpy as jnp
from jax import lax
from jax.sharding import PartitionSpec as P

E = 8


def on_device(
    tokens,
    norm_gain,
    eraser_mean,
    eraser_in,
    eraser_out,
    router,
    expert_ids,
    slots,
    w_gate,
    w_up,
    w_down,
):
    highest = lax.Precision.HIGHEST
    part_count = lax.axis_size("dp") // E
    tok_rows = tokens.shape[0]
    capacity = 3 * tok_rows // 8
    width = tokens.shape[1] * lax.axis_size("tensor")
    values = tokens.astype(jnp.float32)
    gained = values * norm_gain[None, :]
    squares = jnp.sum(values * values, axis=1)
    gained_in = jnp.dot(gained, eraser_in, precision=highest, preferred_element_type=jnp.float32)
    mean_in = jnp.dot(
        eraser_mean[None, :], eraser_in, precision=highest, preferred_element_type=jnp.float32
    )
    router_out = jnp.dot(
        router.T, eraser_out, precision=highest, preferred_element_type=jnp.float32
    )
    routed = jnp.dot(router.T, gained.T, precision=highest, preferred_element_type=jnp.float32)
    rank = eraser_in.shape[1]
    narrow = jnp.concatenate([routed, squares[None, :]], axis=0)
    narrow = jnp.pad(narrow, ((0, 0), (0, rank - tok_rows)))
    packed = lax.psum(jnp.concatenate([gained_in, router_out, mean_in, narrow], axis=0), "tensor")
    gained_in = packed[:tok_rows]
    router_out = packed[tok_rows : tok_rows + E]
    mean_in = packed[tok_rows + E]
    routed = packed[tok_rows + E + 1 : tok_rows + 2 * E + 1, :tok_rows].T
    squares = packed[tok_rows + 2 * E + 1, :tok_rows]
    inv_rms = lax.rsqrt(squares / width + 1e-05)
    projected = inv_rms[:, None] * gained_in - mean_in[None, :]
    cleaned = inv_rms[:, None] * gained - jnp.dot(
        projected, eraser_out.T, precision=highest, preferred_element_type=jnp.float32
    )
    logits = inv_rms[:, None] * routed - jnp.dot(
        projected, router_out.T, precision=highest, preferred_element_type=jnp.float32
    )
    erased = cleaned.astype(jnp.bfloat16)
    chosen = (expert_ids[:, :, None] == jnp.arange(E, dtype=jnp.int32)[None, None, :]).astype(
        jnp.float32
    )
    picked = jnp.sum(chosen * logits[:, None, :], axis=2)
    first_gate = jax.nn.sigmoid(picked[:, 0] - picked[:, 1])
    gate_pair = jnp.stack([first_gate, 1.0 - first_gate], axis=1)
    kept_mask = slots < capacity
    target = expert_ids * capacity + slots
    columns = jnp.arange(E * capacity, dtype=jnp.int32)
    match = ((target[:, :, None] == columns[None, None, :]) & kept_mask[:, :, None]).astype(
        jnp.float32
    )
    placing = jnp.sum(match, axis=1).T.astype(jnp.bfloat16)
    weights = jnp.sum(match * gate_pair[:, :, None], axis=1)
    filled = jnp.dot(placing, erased, preferred_element_type=jnp.float32).astype(jnp.bfloat16)
    received = lax.all_to_all(
        jnp.repeat(filled.reshape(E, capacity, erased.shape[1]), part_count, axis=0),
        "dp",
        split_axis=0,
        concat_axis=0,
        tiled=True,
    )
    received = lax.all_gather(received, "tensor", axis=2, tiled=True)
    sources, count, features = received.shape
    flat_rows = received.reshape(sources * count, features)
    gate_act = jnp.dot(flat_rows, w_gate[0], preferred_element_type=jnp.float32)
    up_act = jnp.dot(flat_rows, w_up[0], preferred_element_type=jnp.float32)
    hidden = (jax.nn.silu(gate_act) * up_act).astype(jnp.bfloat16)
    outputs = (
        jnp.dot(hidden, w_down[0], preferred_element_type=jnp.float32)
        .reshape(sources, count, features)
        .astype(jnp.bfloat16)
    )
    reduced = lax.psum_scatter(outputs, "tensor", scatter_dimension=2, tiled=True)
    returned = lax.all_to_all(reduced, "dp", split_axis=0, concat_axis=0, tiled=True)
    summed = jnp.sum(
        returned.astype(jnp.float32).reshape(E, part_count, capacity, returned.shape[2]), axis=1
    ).reshape(E * capacity, returned.shape[2])
    mixed = jnp.dot(weights, summed, precision=highest, preferred_element_type=jnp.float32)
    return mixed.astype(jnp.bfloat16)


def solution(mesh):
    in_specs = (
        P("dp", "tensor"),
        P("tensor"),
        P("tensor"),
        P("tensor", None),
        P("tensor", None),
        P("tensor", None),
        P("dp", None),
        P("dp", None),
        P("dp", None, "tensor"),
        P("dp", None, "tensor"),
        P("dp", "tensor", None),
    )
    out_specs = P("dp", "tensor")
    return jax.shard_map(
        on_device, mesh=mesh, in_specs=in_specs, out_specs=out_specs, check_vma=False
    )
```

profile of v0, /device:TPU:0, one launch (start us, length us, event | category | flops | bytes accessed | tf_op | source)
XLA Modules:
  0.0 159.8 jit_solution(10361582863395513640)
XLA Ops:
  6.5 0.0 copy-start
  6.5 0.0 copy-start.3
  6.5 0.0 copy-start.2
  6.5 0.0 all-gather.2.cloned.1.call-start
  6.5 1.1 fusion.18
  7.6 1.4 fusion.36
  9.1 1.6 fusion.17
  10.6 1.2 convolution_bitcast_fusion
  11.8 0.0 copy-done
  11.8 1.2 fusion.35
  13.1 13.2 %psum.7 = f32[82,128]{1,0:T(8,128)S(1)} all-reduce(f32[82,128]{1,0:T(8,128)S(1)} %pad_maximum_fusion), channel_id=1, replica_groups=mesh['dp'=8,'tensor'=4] {'tensor'}, use_global_device_ids=true, to_apply=%region_1.2 | all-reduce | flops 10496 | bytes 83968 | tf_op jit(solution)/shard_map/psum | solution.py:41
  26.3 0.2 convolution_subtract_fusion.1
  26.5 1.6 %fusion.15 = bf16[64,1024]{1,0:T(8,128)(2,1)S(1)} fusion(f32[1024,128]{1,0:T(8,128)S(1)} %copy-done, bf16[64,1024]{1,0:T(8,128)(2,1)} %param.11, f32[64]{0:T(128)S(1)} %fusion.34, f32[1024]{0:T(1024)} %param.12, f32[82,128]{1,0:T(8,128)S(1)} %psum.7, f32[128]{0:T(128)S(1)} %slice_bitcast_fusion), kind=kOutput, calls=%fused_computation.11 | convolution fusion | flops 101007360 | bytes 824832 | tf_op jit(solution)/shard_map/dot_general | solution.py:49
  28.2 0.0 copy-done.3
  28.2 0.0 copy-done.2
  28.3 0.1 convert_reduce_fusion
  28.4 0.3 convolution_convert_fusion
  28.7 16.7 %all_to_all.10 = bf16[8,24,1024]{2,1,0:T(8,128)(2,1)} all-to-all(bf16[8,24,1024]{2,1,0:T(8,128)(2,1)S(1)} %bitcast.48), channel_id=1, replica_groups=mesh['dp'=8,'tensor'=4] {'dp'}, dimensions={0} | all-to-all | bytes 786432 | tf_op jit(solution)/shard_map/all_to_all | solution.py:71
  45.4 0.0 all-gather.2.cloned.1.call-update
  45.4 0.0 reduce-scatter.2.cloned.1.call-start
  45.5 18.7 %all-gather.2.cloned.1.call-done = bf16[8,24,4096]{2,1,0:T(8,128)(2,1)} async-done(((bf16[8,24,1024]{2,1,0:T(8,128)(2,1)}), bf16[8,24,4096]{2,1,0:T(8,128)(2,1)}) %all-gather.2.cloned.1.call-update) | async-done | bytes 1572880 | tf_op jit(solution)/shard_map/all_gather | solution.py:78
  64.2 0.0 copy-start.4
  64.2 15.9 %fusion.4 = f32[192,3584]{1,0:T(8,128)S(1)} fusion(bf16[192,4096]{1,0:T(8,128)(2,1)} %bitcast.51, bf16[1,4096,3584]{2,1,0:T(8,128)(2,1)} %param.19), kind=kOutput, calls=%fused_computation.4 | convolution fusion | flops 5637144576 | bytes 33685504 | tf_op jit(solution)/shard_map/dot_general | solution.py:81
  80.1 0.0 copy-done.4
  80.1 12.5 %fusion.9 = bf16[192,3584]{1,0:T(8,128)(2,1)S(1)} fusion(bf16[192,4096]{1,0:T(8,128)(2,1)S(1)} %bitcast.52, bf16[1,4096,3584]{2,1,0:T(8,128)(2,1)} %param.20, f32[192,3584]{1,0:T(8,128)S(1)} %fusion.4), kind=kOutput, calls=%fused_computation.7 | convolution fusion | flops 5641273344 | bytes 35061760 | tf_op jit(solution)/shard_map/dot_general | solution.py:82
  92.6 0.0 copy-start.1
  92.6 13.8 %fusion.12 = bf16[8,24,4096]{2,1,0:T(8,128)(2,1)} fusion(bf16[8,24,3584]{2,1,0:T(8,128)(2,1)S(1)} %bitcast.53, bf16[1,3584,4096]{2,1,0:T(8,128)(2,1)} %param.21), kind=kOutput, calls=%fused_computation.8 | convolution fusion | flops 5637931008 | bytes 32309248 | tf_op jit(solution)/shard_map/dot_general | solution.py:85
  106.4 0.0 reduce-scatter.2.cloned.1.call-update
  106.4 28.1 %reduce-scatter.2.cloned.1.call-done = bf16[8,24,1024]{2,1,0:T(8,128)(2,1)} async-done(((bf16[8,24,4096]{2,1,0:T(8,128)(2,1)}), bf16[8,24,1024]{2,1,0:T(8,128)(2,1)}) %reduce-scatter.2.cloned.1.call-update) | async-done | bytes 393232 | tf_op jit(solution)/shard_map/reduce_scatter | solution.py:89
  134.6 17.4 %all_to_all.11 = bf16[8,24,1024]{2,1,0:T(8,128)(2,1)S(1)} all-to-all(bf16[8,24,1024]{2,1,0:T(8,128)(2,1)} %reduce-scatter.2.cloned.1.call-done), channel_id=1, replica_groups=mesh['dp'=8,'tensor'=4] {'dp'}, dimensions={0} | all-to-all | bytes 786432 | tf_op jit(solution)/shard_map/all_to_all | solution.py:90
  152.0 1.0 convolution_convert_fusion.1
  153.0 0.0 copy-done.1
  (9 shorter events, 0.1 us)
Async XLA Ops:
  6.5 5.3 %copy-start = (f32[1024,128]{1,0:T(8,128)S(1)}, f32[1024,128]{1,0:T(8,128)}, u32[]{:S(2)}) copy-start(f32[1024,128]{1,0:T(8,128)} %param.15) | copy-start | bytes 1572868
  6.5 21.6 %copy-start.3 = (s32[64,2]{0,1:T(2,128)S(1)}, s32[64,2]{0,1:T(2,128)}, u32[]{:S(2)}) copy-start(s32[64,2]{0,1:T(2,128)} %param.18) | copy-start | bytes 1540
  6.5 21.7 %copy-start.2 = (s32[64,2]{0,1:T(2,128)S(1)}, s32[64,2]{0,1:T(2,128)}, u32[]{:S(2)}) copy-start(s32[64,2]{0,1:T(2,128)} %param.17) | copy-start | bytes 1540
  6.5 57.6 %all-gather.2.cloned.1.call-start = ((), (), s32[]{:S(2)}) async-start(), calls=%async_computation.3 | async-start | bytes 1966080 | tf_op jit(solution)/shard_map/all_gather | solution.py:78
  45.4 89.1 %reduce-scatter.2.cloned.1.call-start = ((), (), s32[]{:S(2)}) async-start(), calls=%async_computation.4 | async-start | bytes 1966080 | tf_op jit(solution)/shard_map/reduce_scatter | solution.py:89
  64.2 15.9 %copy-start.4 = (bf16[8,24,4096]{2,1,0:T(8,128)(2,1)S(1)}, bf16[8,24,4096]{2,1,0:T(8,128)(2,1)}, u32[]{:S(2)}) copy-start(bf16[8,24,4096]{2,1,0:T(8,128)(2,1)} %all-gather.2.cloned.1.call-done) | copy-start | bytes 4718596
  92.6 60.4 %copy-start.1 = (f32[1024,128]{1,0:T(8,128)S(1)}, f32[1024,128]{1,0:T(8,128)}, u32[]{:S(2)}) copy-start(f32[1024,128]{1,0:T(8,128)} %param.15) | copy-start | bytes 1572868
Sparse Core Ops, SparseCore 0:
  45.6 18.5 all-gather.1
  106.5 27.9 reduce-scatter.1
where the time goes:
time: 160 us
  matrix products  50.6 us (32%)
  blocking collectives  47.4 us (30%)
  waiting for transfers between devices  46.9 us (29%)
  between operations  13.5 us (8%)
    reduce_scatter x1, waiting for transfers between devices, on_device(): lax.psum_scatter(outputs, 'tensor', scatter_dimension=2, tiled=True)  28.1 us
    all_gather x1, waiting for transfers between devices, on_device(): received = lax.all_gather(received, 'tensor', axis=2, tiled=True)  18.7 us
    all_to_all x1, blocking collectives, on_device(): lax.all_to_all(reduced, 'dp', split_axis=0, concat_axis=0, tiled=True)  17.4 us
    all_to_all x1, blocking collectives, on_device(): lax.all_to_all(jnp.repeat(filled.reshape(E, capacity, erased.shape[1]), p...  16.7 us
    dot_general x1, matrix products, on_device(): gate_act = jnp.dot(flat_rows, w_gate[0], preferred_element_type=jnp.float32)  15.9 us
    dot_general x1, matrix products, on_device(): jnp.dot(hidden, w_down[0], preferred_element_type=jnp.float32)  13.8 us
    psum x1, blocking collectives, on_device(): lax.psum(jnp.concatenate([gained_in, router_out, mean_in, narrow], axis=0...  13.2 us
    dot_general x1, matrix products, on_device(): up_act = jnp.dot(flat_rows, w_up[0], preferred_element_type=jnp.float32)  12.5 us
  transfers between devices with their start and end apart: 2, of which 2 were waited for; matrix products, arithmetic and copies ran while one was open for 0% of the time, Pallas kernels for 0%

commit v1 on v0

--- a/solution.py
+++ b/solution.py
@@ -38,7 +38,10 @@
     rank = eraser_in.shape[1]
     narrow = jnp.concatenate([routed, squares[None, :]], axis=0)
     narrow = jnp.pad(narrow, ((0, 0), (0, rank - tok_rows)))
-    packed = lax.psum(jnp.concatenate([gained_in, router_out, mean_in, narrow], axis=0), "tensor")
+    packed = jnp.sum(
+        lax.all_gather(jnp.concatenate([gained_in, router_out, mean_in, narrow], axis=0), "tensor"),
+        axis=0,
+    )
     gained_in = packed[:tok_rows]
     router_out = packed[tok_rows : tok_rows + E]
     mean_in = packed[tok_rows + E]

time: 160 us -> 155 us (0.969)
  blocking collectives: 47.4 us -> 42.7 us
    psum x1 -> x0, blocking collectives: 13.2 us -> none  [on_device(): lax.psum(jnp.concatenate([gained_in, router_out, mean_in, narrow], axis=0...]
    all_gather x0 -> x1, blocking collectives: none -> 6.81 us  [on_device(): lax.all_gather(jnp.concatenate([gained_in, router_out, mean_in, narrow],...]
    all_to_all x1, blocking collectives: 16.7 us -> 18.5 us  [on_device(): lax.all_to_all(jnp.repeat(filled.reshape(E, capacity, erased.shape[1]), p...]
where the time goes in v1:
time: 155 us
  matrix products  50.4 us (33%)
  waiting for transfers between devices  46.6 us (30%)
  blocking collectives  42.7 us (28%)
  between operations  13.5 us (9%)
    reduce_scatter x1, waiting for transfers between devices, on_device(): lax.psum_scatter(outputs, 'tensor', scatter_dimension=2, tiled=True)  28.1 us
    all_to_all x1, blocking collectives, on_device(): lax.all_to_all(jnp.repeat(filled.reshape(E, capacity, erased.shape[1]), p...  18.5 us
    all_gather x1, waiting for transfers between devices, on_device(): received = lax.all_gather(received, 'tensor', axis=2, tiled=True)  18.4 us
    all_to_all x1, blocking collectives, on_device(): lax.all_to_all(reduced, 'dp', split_axis=0, concat_axis=0, tiled=True)  17.4 us
    dot_general x1, matrix products, on_device(): gate_act = jnp.dot(flat_rows, w_gate[0], preferred_element_type=jnp.float32)  15.9 us
    dot_general x1, matrix products, on_device(): jnp.dot(hidden, w_down[0], preferred_element_type=jnp.float32)  13.8 us
    dot_general x1, matrix products, on_device(): up_act = jnp.dot(flat_rows, w_up[0], preferred_element_type=jnp.float32)  12.5 us
    all_gather x1, blocking collectives, on_device(): lax.all_gather(jnp.concatenate([gained_in, router_out, mean_in, narrow],...  6.81 us
  transfers between devices with their start and end apart: 2, of which 2 were waited for; matrix products, arithmetic and copies ran while one was open for 0% of the time, Pallas kernels for 0%

profile of v1, /device:TPU:0, one launch (start us, length us, event | category | flops | bytes accessed | tf_op | source)
XLA Modules:
  0.0 154.8 jit_solution(17050761935827041043)
XLA Ops:
  6.5 0.0 copy-start
  6.5 0.0 copy-start.2
  6.5 0.0 copy-start.4
  6.5 0.0 all-gather.4.cloned.1.call-start
  6.6 1.1 fusion.18
  7.7 1.4 fusion.36
  9.1 1.6 %fusion.17 = f32[64,128]{1,0:T(8,128)S(1)} fusion(f32[1024,128]{1,0:T(8,128)} %param.14, bf16[64,1024]{1,0:T(8,128)(2,1)} %param.11, f32[1024]{0:T(1024)} %param.12), kind=kOutput, calls=%fused_computation.18 | convolution fusion | flops 100794368 | bytes 692224 | tf_op jit(solution)/shard_map/dot_general | solution.py:30
  10.7 1.2 convolution_bitcast_fusion
  11.9 0.0 copy-done
  11.9 1.2 fusion.35
  13.1 6.8 %all-gather.1 = f32[4,82,128]{2,1,0:T(8,128)S(1)} all-gather(f32[1,82,128]{2,1,0:T(8,128)S(1)} %maximum_bitcast_fusion), channel_id=2, replica_groups=mesh['dp'=8,'tensor'=4] {'tensor'}, dimensions={0}, use_global_device_ids=true | all-gather | bytes 209920 | tf_op jit(solution)/shard_map/all_gather | solution.py:42
  19.9 0.2 convolution_subtract_fusion.1
  20.2 0.0 copy-done.2
  20.2 1.4 fusion.15
  21.6 0.0 copy-done.4
  21.6 0.0 copy-done.3
  21.7 0.1 convert_reduce_fusion
  21.8 0.3 convolution_convert_fusion
  22.1 18.5 %all_to_all.10 = bf16[8,24,1024]{2,1,0:T(8,128)(2,1)} all-to-all(bf16[8,24,1024]{2,1,0:T(8,128)(2,1)S(1)} %bitcast.50), channel_id=1, replica_groups=mesh['dp'=8,'tensor'=4] {'dp'}, dimensions={0} | all-to-all | bytes 786432 | tf_op jit(solution)/shard_map/all_to_all | solution.py:74
  40.6 0.0 all-gather.4.cloned.1.call-update
  40.6 0.0 reduce-scatter.2.cloned.1.call-start
  40.7 18.4 %all-gather.4.cloned.1.call-done = bf16[8,24,4096]{2,1,0:T(8,128)(2,1)} async-done(((bf16[8,24,1024]{2,1,0:T(8,128)(2,1)}), bf16[8,24,4096]{2,1,0:T(8,128)(2,1)}) %all-gather.4.cloned.1.call-update) | async-done | bytes 1572880 | tf_op jit(solution)/shard_map/all_gather | solution.py:81
  59.1 15.9 %fusion.4 = f32[192,3584]{1,0:T(8,128)S(1)} fusion(bf16[192,4096]{1,0:T(8,128)(2,1)} %bitcast.53, bf16[1,4096,3584]{2,1,0:T(8,128)(2,1)} %param.19), kind=kOutput, calls=%fused_computation.4 | convolution fusion | flops 5637144576 | bytes 33685504 | tf_op jit(solution)/shard_map/dot_general | solution.py:84
  75.0 0.0 copy-done.5
  75.0 12.5 %fusion.9 = bf16[192,3584]{1,0:T(8,128)(2,1)S(1)} fusion(bf16[192,4096]{1,0:T(8,128)(2,1)S(1)} %bitcast.54, bf16[1,4096,3584]{2,1,0:T(8,128)(2,1)} %param.20, f32[192,3584]{1,0:T(8,128)S(1)} %fusion.4), kind=kOutput, calls=%fused_computation.7 | convolution fusion | flops 5641273344 | bytes 35061760 | tf_op jit(solution)/shard_map/dot_general | solution.py:85
  87.5 0.0 copy-start.1
  87.6 13.8 %fusion.12 = bf16[8,24,4096]{2,1,0:T(8,128)(2,1)} fusion(bf16[8,24,3584]{2,1,0:T(8,128)(2,1)S(1)} %bitcast.55, bf16[1,3584,4096]{2,1,0:T(8,128)(2,1)} %param.21), kind=kOutput, calls=%fused_computation.8 | convolution fusion | flops 5637931008 | bytes 32309248 | tf_op jit(solution)/shard_map/dot_general | solution.py:88
  101.3 0.0 reduce-scatter.2.cloned.1.call-update
  101.4 28.1 %reduce-scatter.2.cloned.1.call-done = bf16[8,24,1024]{2,1,0:T(8,128)(2,1)} async-done(((bf16[8,24,4096]{2,1,0:T(8,128)(2,1)}), bf16[8,24,1024]{2,1,0:T(8,128)(2,1)}) %reduce-scatter.2.cloned.1.call-update) | async-done | bytes 393232 | tf_op jit(solution)/shard_map/reduce_scatter | solution.py:92
  129.5 17.4 %all_to_all.11 = bf16[8,24,1024]{2,1,0:T(8,128)(2,1)S(1)} all-to-all(bf16[8,24,1024]{2,1,0:T(8,128)(2,1)} %reduce-scatter.2.cloned.1.call-done), channel_id=1, replica_groups=mesh['dp'=8,'tensor'=4] {'dp'}, dimensions={0} | all-to-all | bytes 786432 | tf_op jit(solution)/shard_map/all_to_all | solution.py:93
  146.9 1.0 convolution_convert_fusion.1
  147.9 0.0 copy-done.1
  (12 shorter events, 0.1 us)
Async XLA Ops:
  6.5 5.3 %copy-start = (f32[1024,128]{1,0:T(8,128)S(1)}, f32[1024,128]{1,0:T(8,128)}, u32[]{:S(2)}) copy-start(f32[1024,128]{1,0:T(8,128)} %param.15) | copy-start | bytes 1572868
  6.5 13.6 %copy-start.2 = (bf16[64,1024]{1,0:T(8,128)(2,1)S(1)}, bf16[64,1024]{1,0:T(8,128)(2,1)}, u32[]{:S(2)}) copy-start(bf16[64,1024]{1,0:T(8,128)(2,1)} %param.11) | copy-start | bytes 393220
  6.5 15.0 %copy-start.4 = (s32[64,2]{0,1:T(2,128)S(1)}, s32[64,2]{0,1:T(2,128)}, u32[]{:S(2)}) copy-start(s32[64,2]{0,1:T(2,128)} %param.18) | copy-start | bytes 1540
  6.5 15.1 %copy-start.3 = (s32[64,2]{0,1:T(2,128)S(1)}, s32[64,2]{0,1:T(2,128)}, u32[]{:S(2)}) copy-start(s32[64,2]{0,1:T(2,128)} %param.17) | copy-start | bytes 1540
  6.5 52.6 %all-gather.4.cloned.1.call-start = ((), (), s32[]{:S(2)}) async-start(), calls=%async_computation.3 | async-start | bytes 1966080 | tf_op jit(solution)/shard_map/all_gather | solution.py:81
  40.6 88.9 %reduce-scatter.2.cloned.1.call-start = ((), (), s32[]{:S(2)}) async-start(), calls=%async_computation.4 | async-start | bytes 1966080 | tf_op jit(solution)/shard_map/reduce_scatter | solution.py:92
  59.1 15.9 %copy-start.5 = (bf16[8,24,4096]{2,1,0:T(8,128)(2,1)S(1)}, bf16[8,24,4096]{2,1,0:T(8,128)(2,1)}, u32[]{:S(2)}) copy-start(bf16[8,24,4096]{2,1,0:T(8,128)(2,1)} %all-gather.4.cloned.1.call-done) | copy-start | bytes 4718596
  87.5 60.4 %copy-start.1 = (f32[1024,128]{1,0:T(8,128)S(1)}, f32[1024,128]{1,0:T(8,128)}, u32[]{:S(2)}) copy-start(f32[1024,128]{1,0:T(8,128)} %param.15) | copy-start | bytes 1572868
Sparse Core Ops, SparseCore 0:
  40.7 18.3 all-gather.3
  101.5 27.9 reduce-scatter.1
